TPU v7x, 32 devices: a whole 2x2x4 slice. The times are simulated.
32 devices in a mesh: bag: 4 (over x, core), sp: 8 (over z, y).
Axes of the slice: x: 2, y: 2, z: 4, core: 2. Of those that a mesh axis runs over, the one named last changes fastest.
Arguments:
- tokens: bfloat16 [8192, 1152], P(('bag', 'sp')), may hold values from -8 to 8
- row_seq: int32 [8192], P(('bag', 'sp')), may hold values from 0 to 3, as said below
- modulation: float32 [4, 6, 1152], replicated, may hold values from -4 to 4
- w_qkv: bfloat16 [1152, 3456], replicated, may hold values from -1 to 1
- w_out: bfloat16 [1152, 1152], replicated, may hold values from -0.1875 to 0.1875
- w_fc1: bfloat16 [1152, 2304], replicated, may hold values from -0.1875 to 0.1875
- w_fc2: bfloat16 [2304, 1152], replicated, may hold values from -0.125 to 0.125
Outputs:
- output: bfloat16 [8192, 1152], P(('bag', 'sp'))
Inputs may be any that keep to these rules, and one draw needn't show every extreme that they name: `row_seq`: rows 2m and 2m + 1 belong to the same sequence. Sequence s lies in bag s. Of one device's 256 rows at most 80 lie in any one bag, and on every device exactly 80 lie in one bag. Every sequence has rows.
All inputs are finite; a program needn't handle non-finite values.
Results may differ from a plain program's by a relative error of at most 0.0095.
Values may be sent and summed in bfloat16 or wider, within the bound.
No kernel may reach another device: no remote copies, remote signals or barrier semaphores. Data moves between devices by JAX's collectives and lax.ppermute only.
A program may use at most 128 MiB of HBM per device.

v0:
```python
import math
import jax
import jax.numpy as jnp
from jax import lax
from jax.sharding import PartitionSpec as P

HD = 72
SEQ_BAG = 1
EPS = 1e-06


def layer_norm(values):
    center = values - jnp.mean(values, axis=-1, keepdims=True)
    spread = jnp.mean(center * center, axis=-1, keepdims=True)
    return center * lax.rsqrt(spread + EPS)


def lookup(seq_codes, modulation):
    seq_total = modulation.shape[0]
    one_hot = (seq_codes[:, None] == jnp.arange(seq_total, dtype=jnp.int32)[None, :]).astype(
        jnp.float32
    )
    table_rows = modulation.reshape(seq_total, -1)
    picked = jnp.dot(
        one_hot, table_rows, precision=lax.Precision.HIGHEST, preferred_element_type=jnp.float32
    )
    return picked.reshape(seq_codes.shape[0], 6, -1)


def project(source_rows, mods, w_qkv):
    normed = (layer_norm(source_rows.astype(jnp.float32)) * (1.0 + mods[:, 1]) + mods[:, 0]).astype(
        jnp.bfloat16
    )
    return jnp.dot(normed, w_qkv, preferred_element_type=jnp.float32).astype(jnp.bfloat16)


def attend(packed, seq_codes):
    key_count = packed.shape[0]
    local_width = packed.shape[2]
    head_local = local_width // HD
    queries = packed[:, 0].reshape(key_count, head_local, HD)
    key_rows = packed[:, 1].reshape(key_count, head_local, HD)
    values = packed[:, 2].reshape(key_count, head_local, HD)
    block_size = math.gcd(key_count, 512)
    score_scale = 1.0 / math.sqrt(HD)

    def one_block(block_index):
        first_row = block_index * block_size
        query_part = lax.dynamic_slice_in_dim(queries, first_row, block_size, 0)
        query_seq = lax.dynamic_slice_in_dim(seq_codes, first_row, block_size, 0)
        scores = (
            jnp.einsum("qhd,khd->hqk", query_part, key_rows, preferred_element_type=jnp.float32)
            * score_scale
        )
        allowed = query_seq[:, None] == seq_codes[None, :]
        scores = jnp.where(allowed[None], scores, -jnp.inf)
        row_max = jnp.max(scores, axis=-1, keepdims=True)
        raised = jnp.exp(scores - row_max)
        denominator = jnp.sum(raised, axis=-1)
        probs = raised.astype(jnp.bfloat16)
        mixed_rows = jnp.einsum("hqk,khd->qhd", probs, values, preferred_element_type=jnp.float32)
        mixed_rows = mixed_rows / jnp.transpose(denominator)[:, :, None]
        return mixed_rows.astype(jnp.bfloat16).reshape(block_size, local_width)

    blocks = lax.map(one_block, jnp.arange(key_count // block_size, dtype=jnp.int32))
    return blocks.reshape(key_count, local_width)


def finish(residual, attended, mods, w_out, w_fc1, w_fc2):
    branch = jnp.dot(attended, w_out, preferred_element_type=jnp.float32)
    hidden = (residual.astype(jnp.float32) + mods[:, 2] * branch).astype(jnp.bfloat16)
    normed = (layer_norm(hidden.astype(jnp.float32)) * (1.0 + mods[:, 4]) + mods[:, 3]).astype(
        jnp.bfloat16
    )
    active = jax.nn.gelu(
        jnp.dot(normed, w_fc1, preferred_element_type=jnp.float32), approximate=True
    ).astype(jnp.bfloat16)
    return (
        hidden.astype(jnp.float32)
        + mods[:, 5] * jnp.dot(active, w_fc2, preferred_element_type=jnp.float32)
    ).astype(jnp.bfloat16)


def shards(tokens, row_seq, modulation, w_qkv, w_out, w_fc1, w_fc2):
    bag_count = lax.axis_size("bag")
    sp_count = lax.axis_size("sp")
    row_count, model_width = tokens.shape
    capacity = row_count // bag_count * 5 // 4
    slot_count = bag_count * capacity
    local_width = model_width // sp_count
    key_count = sp_count * slot_count
    bag_of = row_seq // SEQ_BAG
    member = (bag_of[:, None] == jnp.arange(bag_count, dtype=jnp.int32)[None, :]).astype(jnp.int32)
    before = jnp.cumsum(member, axis=0) - member
    rank_in = jnp.sum(before * member, axis=1)
    position = bag_of * capacity + rank_in
    source_row = (
        jnp.zeros((slot_count,), jnp.int32).at[position].set(jnp.arange(row_count, dtype=jnp.int32))
    )
    filled = jnp.zeros((slot_count,), jnp.bool_).at[position].set(True)
    slot_seq = jnp.where(filled, jnp.take(row_seq, source_row), -1)
    send_rows = jnp.where(
        filled[:, None], jnp.take(tokens, source_row, axis=0), jnp.zeros((), jnp.bfloat16)
    )
    arrived, arrived_seq = (
        lax.all_to_all(send_rows, "bag", split_axis=0, concat_axis=0, tiled=True),
        lax.all_to_all(
            slot_seq.astype(jnp.bfloat16), "bag", split_axis=0, concat_axis=0, tiled=True
        ),
    )
    mods = lookup(arrived_seq.astype(jnp.int32), modulation)
    packed = project(arrived, mods, w_qkv).reshape(slot_count, 3, sp_count, local_width)
    code_copies = jnp.broadcast_to(arrived_seq[:, None, None, None], (slot_count, 1, sp_count, 1))
    by_head, head_seq = (
        lax.all_to_all(packed, "sp", split_axis=2, concat_axis=0, tiled=True),
        lax.all_to_all(code_copies, "sp", split_axis=2, concat_axis=0, tiled=True),
    )
    attended = attend(
        by_head.reshape(key_count, 3, local_width), head_seq.reshape(key_count).astype(jnp.int32)
    )
    by_slot = lax.all_to_all(
        attended.reshape(key_count, 1, local_width), "sp", split_axis=0, concat_axis=1, tiled=True
    )
    finished = finish(arrived, by_slot.reshape(slot_count, model_width), mods, w_out, w_fc1, w_fc2)
    returned = lax.all_to_all(finished, "bag", split_axis=0, concat_axis=0, tiled=True)
    return jnp.take(returned, position, axis=0)


def solution(mesh):
    placed = (P(("bag", "sp"), None), P(("bag", "sp")), P(), P(), P(), P(), P())
    return jax.shard_map(
        shards, mesh=mesh, in_specs=placed, out_specs=P(("bag", "sp"), None), check_vma=False
    )
```

profile of v0, /device:TPU:0, one launch (start us, length us, event | category | flops | bytes accessed | tf_op | source)
XLA Modules:
  0.0 309.8 jit_solution(6032710517958751895)
XLA Ops:
  0.0 0.8 compare_convert_fusion
  0.8 1.2 reduce-window.6
  2.4 0.7 fusion.65
  3.1 0.7 compare_and_fusion.1
  3.8 1.4 scatter_custom_fusion.1
  5.3 3.6 %gather_fusion.1 = s32[320]{0:T(512)S(1)} fusion(s32[256]{0:T(256)} %param.10, s32[1024]{0:T(1024)S(1)} %pad_clamp_fusion.1), kind=kCustom, calls=%fused_computation.1 | custom fusion | bytes 3840 | tf_op jit(solution)/shard_map/jit(_take)/gather | solution.py:101
  8.9 1.5 scatter_custom_fusion
  11.1 4.2 %all-to-all-start.1 = ((bf16[4,80,1]{1,2,0:T(2,128)(2,1)}), bf16[4,80,1]{1,2,0:T(2,128)(2,1)S(1)}, u32[]{:S(2)}, u32[]{:S(2)}) async-start(bf16[4,80,1]{1,2,0:T(2,128)(2,1)} %all_to_all.63), calls=%async_computation.1 | async-start | bytes 4096 | tf_op jit(solution)/shard_map/all_to_all | solution.py:107
  15.5 2.7 gather_fusion
  18.2 2.3 select_select_fusion
  20.5 3.5 %all-to-all-start = ((bf16[4,80,1152]{2,1,0:T(8,128)(2,1)}), bf16[4,80,1152]{2,1,0:T(8,128)(2,1)S(1)}, u32[]{:S(2)}, u32[]{:S(2)}) async-start(bf16[4,80,1152]{2,1,0:T(8,128)(2,1)} %select_select_fusion), calls=%async_computation | async-start | bytes 1474560 | tf_op jit(solution)/shard_map/all_to_all | solution.py:106
  25.3 0.7 reshape.218
  26.0 6.2 %fusion.59 = f32[320,6,1152]{2,0,1:T(8,128)} fusion(f32[4,6,1152]{2,0,1:T(4,128)S(1)} %copy-done.5, s32[320]{0:T(512)S(1)} %convert_element_type.74), kind=kOutput, calls=%fused_computation.68 | convolution fusion | flops 106169600 | bytes 8959232 | tf_op jit(solution)/shard_map/dot_general | solution.py:24
  32.2 2.9 all-to-all-done
  35.0 6.3 %all-to-all-start.2 = ((bf16[8,2,160]{2,1,0:T(2,128)(2,1)}), bf16[8,2,160]{2,1,0:T(2,128)(2,1)S(1)}, u32[]{:S(2)}, u32[]{:S(2)}) async-start(bf16[8,2,160]{2,1,0:T(2,128)(2,1)} %reshape.218), calls=%async_computation.2 | async-start | bytes 16384 | tf_op jit(solution)/shard_map/all_to_all | solution.py:116
  42.1 2.2 fusion.39
  44.3 7.7 %convolution_convert_fusion = bf16[320,3456]{1,0:T(8,128)(2,1)} fusion(bf16[320,1152]{1,0:T(8,128)(2,1)S(1)} %fusion.39, bf16[1152,3456]{1,0:T(8,128)(2,1)} %param.12), kind=kOutput, calls=%fused_computation.22 | convolution fusion | flops 2549145600 | bytes 10911744 | tf_op jit(solution)/shard_map/dot_general | solution.py:34
  52.0 4.4 %copy.20 = bf16[320,3456]{0,1:T(8,128)(2,1)} copy(bf16[320,3456]{1,0:T(8,128)(2,1)} %convolution_convert_fusion) | data formatting | bytes 4423680 | tf_op jit(solution)/shard_map/convert_element_type | solution.py:34
  56.4 3.6 %copy.21 = bf16[320,3,8,144]{0,3,1,2:T(8,128)(2,1)} copy(bf16[320,3,8,144]{0,3,2,1:T(8,128)(2,1)} %bitcast.141) | data formatting | bytes 4423680 | tf_op jit(solution)/shard_map/reshape | solution.py:112
  60.0 6.0 %all-to-all-start.3 = ((bf16[320,3,8,144]{0,3,1,2:T(8,128)(2,1)}), bf16[320,3,8,144]{0,3,1,2:T(8,128)(2,1)}, u32[]{:S(2)}, u32[]{:S(2)}) async-start(bf16[320,3,8,144]{0,3,1,2:T(8,128)(2,1)} %copy.21), calls=%async_computation.3 | async-start | bytes 5308416 | tf_op jit(solution)/shard_map/all_to_all | solution.py:115
  66.2 59.2 %all-to-all-done.3 = bf16[320,3,8,144]{0,3,1,2:T(8,128)(2,1)} async-done(((bf16[320,3,8,144]{0,3,1,2:T(8,128)(2,1)}), bf16[320,3,8,144]{0,3,1,2:T(8,128)(2,1)}, u32[]{:S(2)}, u32[]{:S(2)}) %all-to-all-start.3) | async-done | bytes 2211872 | tf_op jit(solution)/shard_map/all_to_all | solution.py:115
  125.4 3.9 %copy.22 = bf16[8,320,3,1,144]{1,0,4,2,3:T(8,128)(2,1)} copy(bf16[8,320,3,1,144]{1,4,2,0,3:T(8,128)(2,1)} %bitcast.20) | data formatting | bytes 4423680 | tf_op jit(solution)/shard_map/all_to_all | solution.py:115
  129.4 5.2 %reshape.161 = bf16[2560,3,144]{0,2,1:T(8,128)(2,1)} reshape(bf16[8,320,3,1,144]{1,0,4,2,3:T(8,128)(2,1)} %copy.22) | data formatting | bytes 4423680 | tf_op jit(solution)/shard_map/reshape | solution.py:119
  134.6 3.0 fusion.76
  137.6 68.0 %while.10 = (s32[]{:T(128)}, bf16[5,512,144]{1,2,0:T(8,128)(2,1)}, s32[5]{0:T(128)S(1)}, s32[2560]{0:T(1024)S(1)}, bf16[2560,2,72]{0,2,1:T(8,128)(2,1)}, /*index...) while((s32[]{:T(128)}, bf16[5,512,144]{1,2,0:T(8,128)(2,1)}, ...), condition=%wide.region_10.11_spmd, body=%wide.region_7.10_spmd.sunk | while | flops 785266688 | bytes 38802096 | solution.py:65
  138.9 0.8 broadcast_compare_fusion.2
  139.7 3.7 %fusion.95 = (f32[2,512]{1,0:T(2,128)S(1)}, f32[2,512,2560]{2,1,0:T(8,128)S(1)}) fusion(pred[512,2560]{1,0:T(8,128)(4,1)S(1)} %broadcast_compare_fusion.2, bf16[2560,2,72]{0,2,1:T(8,128)(2,1)} %get-tuple-element.142, bf16[2560,2,72]{0,2,1:T(8,128)(2,1)} %get-tuple-element.141, s32[]{:T(128)S(6)} %select_n.87), kind=kOutput, calls=%fused_computation.7.clone.1 | convolution fusion | flops 385350656 | bytes 12685316 | tf_op jit(solution)/shard_map/while/body/eval_jaxpr/qhd,khd->hqk/dot_general | solution.py:52
  143.4 3.0 fusion.96
  146.4 4.1 %fusion.97 = bf16[512,2,72]{0,2,1:T(8,128)(2,1)S(1)} fusion(bf16[2560,2,72]{0,2,1:T(8,128)(2,1)} %get-tuple-element.143, f32[2,512,2560]{2,1,0:T(8,128)S(1)} %get-tuple-element.113, f32[2,512]{1,0:T(2,128)S(1)} %get-tuple-element.114, pred[512,2560]{1,0:T(8,128)(4,1)S(1)} %broadcast_compare_fusion.2, f32[512,2]{0,1:T(2,128)S(1)} %bitcast.150), kind=kOutput, calls=%fused_computation.15.clone.1 | convolution fusion | flops 388120576 | bytes 12689408 | tf_op jit(solution)/shard_map/while/body/eval_jaxpr/hqk,khd->qhd/dot_general | solution.py:61
  150.5 0.7 constant_dynamic-update-slice_fusion.2
  152.5 0.8 broadcast_compare_fusion.2
  153.3 3.7 %fusion.95 = (f32[2,512]{1,0:T(2,128)S(1)}, f32[2,512,2560]{2,1,0:T(8,128)S(1)}) fusion(pred[512,2560]{1,0:T(8,128)(4,1)S(1)} %broadcast_compare_fusion.2, bf16[2560,2,72]{0,2,1:T(8,128)(2,1)} %get-tuple-element.142, bf16[2560,2,72]{0,2,1:T(8,128)(2,1)} %get-tuple-element.141, s32[]{:T(128)S(6)} %select_n.87), kind=kOutput, calls=%fused_computation.7.clone.1 | convolution fusion | flops 385350656 | bytes 12685316 | tf_op jit(solution)/shard_map/while/body/eval_jaxpr/qhd,khd->hqk/dot_general | solution.py:52
  157.0 3.0 fusion.96
  160.1 4.1 %fusion.97 = bf16[512,2,72]{0,2,1:T(8,128)(2,1)S(1)} fusion(bf16[2560,2,72]{0,2,1:T(8,128)(2,1)} %get-tuple-element.143, f32[2,512,2560]{2,1,0:T(8,128)S(1)} %get-tuple-element.113, f32[2,512]{1,0:T(2,128)S(1)} %get-tuple-element.114, pred[512,2560]{1,0:T(8,128)(4,1)S(1)} %broadcast_compare_fusion.2, f32[512,2]{0,1:T(2,128)S(1)} %bitcast.150), kind=kOutput, calls=%fused_computation.15.clone.1 | convolution fusion | flops 388120576 | bytes 12689408 | tf_op jit(solution)/shard_map/while/body/eval_jaxpr/hqk,khd->qhd/dot_general | solution.py:61
  164.1 0.7 constant_dynamic-update-slice_fusion.2
  166.1 0.8 broadcast_compare_fusion.2
  166.9 3.7 %fusion.95 = (f32[2,512]{1,0:T(2,128)S(1)}, f32[2,512,2560]{2,1,0:T(8,128)S(1)}) fusion(pred[512,2560]{1,0:T(8,128)(4,1)S(1)} %broadcast_compare_fusion.2, bf16[2560,2,72]{0,2,1:T(8,128)(2,1)} %get-tuple-element.142, bf16[2560,2,72]{0,2,1:T(8,128)(2,1)} %get-tuple-element.141, s32[]{:T(128)S(6)} %select_n.87), kind=kOutput, calls=%fused_computation.7.clone.1 | convolution fusion | flops 385350656 | bytes 12685316 | tf_op jit(solution)/shard_map/while/body/eval_jaxpr/qhd,khd->hqk/dot_general | solution.py:52
  170.6 3.0 fusion.96
  173.7 4.1 %fusion.97 = bf16[512,2,72]{0,2,1:T(8,128)(2,1)S(1)} fusion(bf16[2560,2,72]{0,2,1:T(8,128)(2,1)} %get-tuple-element.143, f32[2,512,2560]{2,1,0:T(8,128)S(1)} %get-tuple-element.113, f32[2,512]{1,0:T(2,128)S(1)} %get-tuple-element.114, pred[512,2560]{1,0:T(8,128)(4,1)S(1)} %broadcast_compare_fusion.2, f32[512,2]{0,1:T(2,128)S(1)} %bitcast.150), kind=kOutput, calls=%fused_computation.15.clone.1 | convolution fusion | flops 388120576 | bytes 12689408 | tf_op jit(solution)/shard_map/while/body/eval_jaxpr/hqk,khd->qhd/dot_general | solution.py:61
  177.7 0.7 constant_dynamic-update-slice_fusion.2
  179.7 0.8 broadcast_compare_fusion.2
  180.5 3.7 %fusion.95 = (f32[2,512]{1,0:T(2,128)S(1)}, f32[2,512,2560]{2,1,0:T(8,128)S(1)}) fusion(pred[512,2560]{1,0:T(8,128)(4,1)S(1)} %broadcast_compare_fusion.2, bf16[2560,2,72]{0,2,1:T(8,128)(2,1)} %get-tuple-element.142, bf16[2560,2,72]{0,2,1:T(8,128)(2,1)} %get-tuple-element.141, s32[]{:T(128)S(6)} %select_n.87), kind=kOutput, calls=%fused_computation.7.clone.1 | convolution fusion | flops 385350656 | bytes 12685316 | tf_op jit(solution)/shard_map/while/body/eval_jaxpr/qhd,khd->hqk/dot_general | solution.py:52
  184.2 3.0 fusion.96
  187.3 4.1 %fusion.97 = bf16[512,2,72]{0,2,1:T(8,128)(2,1)S(1)} fusion(bf16[2560,2,72]{0,2,1:T(8,128)(2,1)} %get-tuple-element.143, f32[2,512,2560]{2,1,0:T(8,128)S(1)} %get-tuple-element.113, f32[2,512]{1,0:T(2,128)S(1)} %get-tuple-element.114, pred[512,2560]{1,0:T(8,128)(4,1)S(1)} %broadcast_compare_fusion.2, f32[512,2]{0,1:T(2,128)S(1)} %bitcast.150), kind=kOutput, calls=%fused_computation.15.clone.1 | convolution fusion | flops 388120576 | bytes 12689408 | tf_op jit(solution)/shard_map/while/body/eval_jaxpr/hqk,khd->qhd/dot_general | solution.py:61
  193.3 0.8 broadcast_compare_fusion.2
  194.1 3.7 %fusion.95 = (f32[2,512]{1,0:T(2,128)S(1)}, f32[2,512,2560]{2,1,0:T(8,128)S(1)}) fusion(pred[512,2560]{1,0:T(8,128)(4,1)S(1)} %broadcast_compare_fusion.2, bf16[2560,2,72]{0,2,1:T(8,128)(2,1)} %get-tuple-element.142, bf16[2560,2,72]{0,2,1:T(8,128)(2,1)} %get-tuple-element.141, s32[]{:T(128)S(6)} %select_n.87), kind=kOutput, calls=%fused_computation.7.clone.1 | convolution fusion | flops 385350656 | bytes 12685316 | tf_op jit(solution)/shard_map/while/body/eval_jaxpr/qhd,khd->hqk/dot_general | solution.py:52
  197.8 3.0 fusion.96
  200.9 4.1 %fusion.97 = bf16[512,2,72]{0,2,1:T(8,128)(2,1)S(1)} fusion(bf16[2560,2,72]{0,2,1:T(8,128)(2,1)} %get-tuple-element.143, f32[2,512,2560]{2,1,0:T(8,128)S(1)} %get-tuple-element.113, f32[2,512]{1,0:T(2,128)S(1)} %get-tuple-element.114, pred[512,2560]{1,0:T(8,128)(4,1)S(1)} %broadcast_compare_fusion.2, f32[512,2]{0,1:T(2,128)S(1)} %bitcast.150), kind=kOutput, calls=%fused_computation.15.clone.1 | convolution fusion | flops 388120576 | bytes 12689408 | tf_op jit(solution)/shard_map/while/body/eval_jaxpr/hqk,khd->qhd/dot_general | solution.py:61
  205.6 2.3 copy.27
  207.9 8.5 %reshape.212 = bf16[2560,1,144]{2,1,0:T(2,128)(2,1)} reshape(bf16[5,512,144]{2,1,0:T(8,128)(2,1)} %copy.27) | data formatting | bytes 1474560 | tf_op jit(solution)/shard_map/reshape;reshape | solution.py:122
  216.5 16.4 %reduce.4 = bf16[2560,144]{1,0:T(8,128)(2,1)} reduce(bf16[2560,1,144]{2,1,0:T(2,128)(2,1)} %reshape.212, bf16[]{:T(256)} %broadcast.160), dimensions={1}, to_apply=%reshape.212.reduce_sub_computation | reduce | bytes 1474562 | tf_op jit(solution)/shard_map/reshape;reshape | solution.py:122
  232.9 4.4 %reshape.220 = bf16[8,2,23040]{2,1,0:T(2,128)(2,1)} reshape(bf16[2560,144]{1,0:T(8,128)(2,1)} %reduce.4) | data formatting | bytes 1474560
  237.3 22.9 %all_to_all.70 = bf16[8,2,23040]{2,1,0:T(2,128)(2,1)S(1)} all-to-all(bf16[8,2,23040]{2,1,0:T(2,128)(2,1)} %reshape.220), channel_id=1, replica_groups=mesh['bag'=4,'sp'=8] {'sp'}, dimensions={0} | all-to-all | bytes 1474560 | tf_op jit(solution)/shard_map/all_to_all | solution.py:121
  260.2 5.3 %reshape.221 = bf16[2560,1,144]{2,1,0:T(2,128)(2,1)} reshape(bf16[8,2,23040]{2,1,0:T(2,128)(2,1)S(1)} %all_to_all.70) | data formatting | bytes 1474560
  265.6 6.1 %copy.25 = bf16[2560,1,144]{0,2,1:T(8,128)(2,1)} copy(bf16[2560,1,144]{2,1,0:T(2,128)(2,1)} %reshape.221) | data formatting | bytes 1474560 | tf_op jit(solution)/shard_map/all_to_all | solution.py:121
  271.6 2.5 all_to_all.58
  274.2 1.3 copy.26
  275.5 2.8 fusion.77
  278.3 1.2 copy-done.4
  279.8 11.4 %fusion.30 = bf16[320,1152]{1,0:T(8,128)(2,1)} fusion(f32[320,1152]{1,0:T(8,128)} %copy-done.4, bf16[2304,1152]{1,0:T(8,128)(2,1)} %param.15, f32[320,6,1152]{2,0,1:T(8,128)} %fusion.59, bf16[1152,2304]{1,0:T(8,128)(2,1)} %param.14, f32[320]{0:T(512)S(1)} %add_rsqrt_fusion, f32[320]{0:T(512)S(1)} %broadcast_multiply_fusion), kind=kOutput, calls=%fused_computation.36 | convolution fusion | flops 3407339520 | bytes 18729472 | tf_op jit(solution)/shard_map/dot_general | solution.py:80
  291.1 3.5 %all-to-all-start.5 = ((bf16[4,80,1152]{2,1,0:T(8,128)(2,1)}), bf16[4,80,1152]{2,1,0:T(8,128)(2,1)S(1)}, u32[]{:S(2)}, u32[]{:S(2)}) async-start(bf16[4,80,1152]{2,1,0:T(8,128)(2,1)} %bitcast.149), calls=%async_computation.5 | async-start | bytes 1474560 | tf_op jit(solution)/shard_map/all_to_all | solution.py:125
  294.6 11.0 %all-to-all-done.5 = bf16[4,80,1152]{2,1,0:T(8,128)(2,1)S(1)} async-done(((bf16[4,80,1152]{2,1,0:T(8,128)(2,1)}), bf16[4,80,1152]{2,1,0:T(8,128)(2,1)S(1)}, u32[]{:S(2)}, u32[]{:S(2)}) %all-to-all-start.5) | async-done | bytes 737312 | tf_op jit(solution)/shard_map/all_to_all | solution.py:125
  305.7 2.1 gather_fusion.2
  307.8 2.0 broadcast_select_fusion
  (60 shorter events, 8.6 us)
Async XLA Ops:
  0.0 275.4 %copy-start = (bf16[1152,1152]{1,0:T(8,128)(2,1)S(1)}, bf16[1152,1152]{1,0:T(8,128)(2,1)}, u32[]{:S(2)}) copy-start(bf16[1152,1152]{1,0:T(8,128)(2,1)} %param.13) | copy-start | bytes 7962628
  0.0 15.5 %copy-start.1 = (bf16[256,1152]{1,0:T(8,128)(2,1)S(1)}, bf16[256,1152]{1,0:T(8,128)(2,1)}, u32[]{:S(2)}) copy-start(bf16[256,1152]{1,0:T(8,128)(2,1)} %param.9) | copy-start | bytes 1769476
  11.1 9.4 %all-to-all-start.1 = ((bf16[4,80,1]{1,2,0:T(2,128)(2,1)}), bf16[4,80,1]{1,2,0:T(2,128)(2,1)S(1)}, u32[]{:S(2)}, u32[]{:S(2)}) async-start(bf16[4,80,1]{1,2,0:T(2,128)(2,1)} %all_to_all.63), calls=%async_computation.1 | async-start | bytes 4096 | tf_op jit(solution)/shard_map/all_to_all | solution.py:107
  18.2 7.8 %copy-start.5 = (f32[4,6,1152]{2,0,1:T(4,128)S(1)}, f32[4,6,1152]{2,0,1:T(4,128)}, u32[]{:S(2)}) copy-start(f32[4,6,1152]{2,0,1:T(4,128)} %param.11) | copy-start | bytes 331780
  20.5 14.6 %all-to-all-start = ((bf16[4,80,1152]{2,1,0:T(8,128)(2,1)}), bf16[4,80,1152]{2,1,0:T(8,128)(2,1)S(1)}, u32[]{:S(2)}, u32[]{:S(2)}) async-start(bf16[4,80,1152]{2,1,0:T(8,128)(2,1)} %select_select_fusion), calls=%async_computation | async-start | bytes 1474560 | tf_op jit(solution)/shard_map/all_to_all | solution.py:106
  35.0 9.3 %copy-start.2 = (bf16[4,80,1152]{2,1,0:T(8,128)(2,1)}, bf16[4,80,1152]{2,1,0:T(8,128)(2,1)S(1)}, u32[]{:S(2)}) copy-start(bf16[4,80,1152]{2,1,0:T(8,128)(2,1)S(1)} %all-to-all-done) | copy-start | bytes 2211844
  35.0 25.0 %all-to-all-start.2 = ((bf16[8,2,160]{2,1,0:T(2,128)(2,1)}), bf16[8,2,160]{2,1,0:T(2,128)(2,1)S(1)}, u32[]{:S(2)}, u32[]{:S(2)}) async-start(bf16[8,2,160]{2,1,0:T(2,128)(2,1)} %reshape.218), calls=%async_computation.2 | async-start | bytes 16384 | tf_op jit(solution)/shard_map/all_to_all | solution.py:116
  60.0 65.4 %all-to-all-start.3 = ((bf16[320,3,8,144]{0,3,1,2:T(8,128)(2,1)}), bf16[320,3,8,144]{0,3,1,2:T(8,128)(2,1)}, u32[]{:S(2)}, u32[]{:S(2)}) async-start(bf16[320,3,8,144]{0,3,1,2:T(8,128)(2,1)} %copy.21), calls=%async_computation.3 | async-start | bytes 5308416 | tf_op jit(solution)/shard_map/all_to_all | solution.py:115
  265.6 9.9 %copy-start.3 = (bf16[4,80,1152]{2,1,0:T(8,128)(2,1)S(1)}, bf16[4,80,1152]{2,1,0:T(8,128)(2,1)}, u32[]{:S(2)}) copy-start(bf16[4,80,1152]{2,1,0:T(8,128)(2,1)} %copy-done.2) | copy-start | bytes 2211844
  278.3 1.2 copy-start.4
  291.1 14.6 %all-to-all-start.5 = ((bf16[4,80,1152]{2,1,0:T(8,128)(2,1)}), bf16[4,80,1152]{2,1,0:T(8,128)(2,1)S(1)}, u32[]{:S(2)}, u32[]{:S(2)}) async-start(bf16[4,80,1152]{2,1,0:T(8,128)(2,1)} %bitcast.149), calls=%async_computation.5 | async-start | bytes 1474560 | tf_op jit(solution)/shard_map/all_to_all | solution.py:125
where the time goes:
time: 312 us; the launch traced here: 310 us
  waiting for transfers between devices  73.2 us (23%)
  local copies, waits for them, and re-layouts  72.6 us (23%)
  matrix products  66.9 us (21%)
  other arithmetic  47.3 us (15%)
  starting transfers between devices  23.5 us (8%)
  blocking collectives  22.9 us (7%)
  loops' own time  3.18 us (1%)
    all_to_all x1, waiting for transfers between devices, shards(): lax.all_to_all(packed, 'sp', split_axis=2, concat_axis=0, tiled=True)  59.2 us
    all_to_all x1, blocking collectives, shards(): lax.all_to_all(attended.reshape(key_count, 1, local_width), 'sp', split_a...  22.9 us
    dot_general x5, matrix products, one_block(): jnp.einsum('hqk,khd->qhd', probs, values, preferred_element_type=jnp.floa...  20.3 us
    dot_general x5, matrix products, one_block(): jnp.einsum('qhd,khd->hqk', query_part, key_rows, preferred_element_type=j...  18.6 us
    another operation x1, other arithmetic, shards(): attended.reshape(key_count, 1, local_width)  16.4 us
    reduce_sum x5, other arithmetic, one_block(): denominator = jnp.sum(raised, axis=-1)  15.2 us
    unnamed x18, local copies, waits for them, and re-layouts  12.2 us
    dot_general x1, matrix products, finish(): jnp.dot(active, w_fc2, preferred_element_type=jnp.float32)  11.4 us
  transfers between devices with their start and end apart: 5, of which 3 were waited for; matrix products, arithmetic and copies ran while one was open for 10% of the time, Pallas kernels for 0%

commit v1 on v0

--- a/solution.py
+++ b/solution.py
@@ -118,8 +118,16 @@
     attended = attend(
         by_head.reshape(key_count, 3, local_width), head_seq.reshape(key_count).astype(jnp.int32)
     )
-    by_slot = lax.all_to_all(
-        attended.reshape(key_count, 1, local_width), "sp", split_axis=0, concat_axis=1, tiled=True
+    by_slot = jnp.concatenate(
+        lax.all_to_all(
+            jnp.stack(
+                jnp.split(attended.reshape(key_count, 1, local_width), lax.axis_size("sp"), axis=0)
+            ),
+            "sp",
+            0,
+            0,
+        ),
+        axis=1,
     )
     finished = finish(arrived, by_slot.reshape(slot_count, model_width), mods, w_out, w_fc1, w_fc2)
     returned = lax.all_to_all(finished, "bag", split_axis=0, concat_axis=0, tiled=True)

time: 312 us -> 281 us (0.901)
  local copies, waits for them, and re-layouts: 72.6 us -> 55.4 us
  other arithmetic: 47.3 us -> 30.9 us
  blocking collectives: 22.9 us -> 26.3 us
    another operation x3 -> x2, other arithmetic: 17.7 us -> 1.24 us  [the longest x1 16.4 us: shards(): attended.reshape(key_count, 1, local_width)]
    all_to_all x3 -> x0, local copies, waits for them, and re-layouts: 9.86 us -> none  [shards(): lax.all_to_all(attended.reshape(key_count, 1, local_width), 'sp', split_a...]
    another operation x2 -> x1, local copies, waits for them, and re-layouts: 10.9 us -> 2.83 us  [shards(): attended.reshape(key_count, 1, local_width)]
    all_to_all x1, blocking collectives: 22.9 us -> 26.3 us  [shards(): lax.all_to_all(jnp.stack(jnp.split(attended.reshape(key_count, 1, local_w...]
    unnamed x18 -> x23, local copies, waits for them, and re-layouts: 12.2 us -> 9.19 us
  transfers between devices with their start and end apart: 5 -> 5, of which waited for: 3 -> 3; matrix products, arithmetic and copies ran while one was open for 10% -> 11% of each run, Pallas kernels for 0% -> 0%
where the time goes in v1:
time: 281 us; the launch traced here: 279 us
  waiting for transfers between devices  73.1 us (26%)
  matrix products  66.9 us (24%)
  local copies, waits for them, and re-layouts  55.4 us (20%)
  other arithmetic  30.9 us (11%)
  blocking collectives  26.3 us (9%)
  starting transfers between devices  23.5 us (8%)
  loops' own time  3.18 us (1%)
    all_to_all x1, waiting for transfers between devices, shards(): lax.all_to_all(packed, 'sp', split_axis=2, concat_axis=0, tiled=True)  59.2 us
    all_to_all x1, blocking collectives, shards(): lax.all_to_all(jnp.stack(jnp.split(attended.reshape(key_count, 1, local_w...  26.3 us
    dot_general x5, matrix products, one_block(): jnp.einsum('hqk,khd->qhd', probs, values, preferred_element_type=jnp.floa...  20.3 us
    dot_general x5, matrix products, one_block(): jnp.einsum('qhd,khd->hqk', query_part, key_rows, preferred_element_type=j...  18.6 us
    reduce_sum x5, other arithmetic, one_block(): denominator = jnp.sum(raised, axis=-1)  15.2 us
    dot_general x1, matrix products, finish(): jnp.dot(active, w_fc2, preferred_element_type=jnp.float32)  11.4 us
    all_to_all x1, waiting for transfers between devices, shards(): lax.all_to_all(finished, 'bag', split_axis=0, concat_axis=0, tiled=True)  11 us
    unnamed x23, local copies, waits for them, and re-layouts  9.19 us
  transfers between devices with their start and end apart: 5, of which 3 were waited for; matrix products, arithmetic and copies ran while one was open for 11% of the time, Pallas kernels for 0%

profile of v1, /device:TPU:0, one launch (start us, length us, event | category | flops | bytes accessed | tf_op | source)
XLA Modules:
  0.0 279.5 jit_solution(6469937358615033665)
XLA Ops:
  0.0 0.8 compare_convert_fusion
  0.8 1.2 reduce-window.6
  2.4 0.7 fusion.73
  3.1 0.7 compare_and_fusion.1
  3.8 1.4 scatter_custom_fusion.1
  5.3 3.6 %gather_fusion.1 = s32[320]{0:T(512)S(1)} fusion(s32[256]{0:T(256)} %param.10, s32[1024]{0:T(1024)S(1)} %pad_clamp_fusion.1), kind=kCustom, calls=%fused_computation.1 | custom fusion | bytes 3840 | tf_op jit(solution)/shard_map/jit(_take)/gather | solution.py:101
  8.9 1.5 scatter_custom_fusion
  11.1 4.2 %all-to-all-start.1 = ((bf16[4,80,1]{1,2,0:T(2,128)(2,1)}), bf16[4,80,1]{1,2,0:T(2,128)(2,1)S(1)}, u32[]{:S(2)}, u32[]{:S(2)}) async-start(bf16[4,80,1]{1,2,0:T(2,128)(2,1)} %all_to_all.53), calls=%async_computation.1 | async-start | bytes 4096 | tf_op jit(solution)/shard_map/all_to_all | solution.py:107
  15.5 2.7 gather_fusion
  18.2 2.3 select_select_fusion
  20.5 3.5 %all-to-all-start = ((bf16[4,80,1152]{2,1,0:T(8,128)(2,1)}), bf16[4,80,1152]{2,1,0:T(8,128)(2,1)S(1)}, u32[]{:S(2)}, u32[]{:S(2)}) async-start(bf16[4,80,1152]{2,1,0:T(8,128)(2,1)} %select_select_fusion), calls=%async_computation | async-start | bytes 1474560 | tf_op jit(solution)/shard_map/all_to_all | solution.py:106
  24.6 0.7 reduce.3
  26.0 6.2 %fusion.67 = f32[320,6,1152]{2,0,1:T(8,128)} fusion(f32[4,6,1152]{2,0,1:T(4,128)S(1)} %copy-done.5, s32[320]{0:T(512)S(1)} %convert_element_type.74), kind=kOutput, calls=%fused_computation.84 | convolution fusion | flops 106169600 | bytes 8959232 | tf_op jit(solution)/shard_map/dot_general | solution.py:24
  32.2 2.8 %all-to-all-done = bf16[4,80,1152]{2,1,0:T(8,128)(2,1)S(1)} async-done(((bf16[4,80,1152]{2,1,0:T(8,128)(2,1)}), bf16[4,80,1152]{2,1,0:T(8,128)(2,1)S(1)}, u32[]{:S(2)}, u32[]{:S(2)}) %all-to-all-start) | async-done | bytes 737312 | tf_op jit(solution)/shard_map/all_to_all | solution.py:106
  35.0 6.3 %all-to-all-start.2 = ((bf16[8,2,160]{2,1,0:T(2,128)(2,1)}), bf16[8,2,160]{2,1,0:T(2,128)(2,1)S(1)}, u32[]{:S(2)}, u32[]{:S(2)}) async-start(bf16[8,2,160]{2,1,0:T(2,128)(2,1)} %reshape.216), calls=%async_computation.2 | async-start | bytes 16384 | tf_op jit(solution)/shard_map/all_to_all | solution.py:116
  42.1 2.2 fusion.39
  44.3 7.7 %convolution_convert_fusion = bf16[320,3456]{1,0:T(8,128)(2,1)} fusion(bf16[320,1152]{1,0:T(8,128)(2,1)S(1)} %fusion.39, bf16[1152,3456]{1,0:T(8,128)(2,1)} %param.12), kind=kOutput, calls=%fused_computation.22 | convolution fusion | flops 2549145600 | bytes 10911744 | tf_op jit(solution)/shard_map/dot_general | solution.py:34
  52.0 4.4 %copy.26 = bf16[320,3456]{0,1:T(8,128)(2,1)} copy(bf16[320,3456]{1,0:T(8,128)(2,1)} %convolution_convert_fusion) | data formatting | bytes 4423680 | tf_op jit(solution)/shard_map/convert_element_type | solution.py:34
  56.4 3.6 %copy.27 = bf16[320,3,8,144]{0,3,1,2:T(8,128)(2,1)} copy(bf16[320,3,8,144]{0,3,2,1:T(8,128)(2,1)} %bitcast.174) | data formatting | bytes 4423680 | tf_op jit(solution)/shard_map/reshape | solution.py:112
  60.0 6.0 %all-to-all-start.3 = ((bf16[320,3,8,144]{0,3,1,2:T(8,128)(2,1)}), bf16[320,3,8,144]{0,3,1,2:T(8,128)(2,1)}, u32[]{:S(2)}, u32[]{:S(2)}) async-start(bf16[320,3,8,144]{0,3,1,2:T(8,128)(2,1)} %copy.27), calls=%async_computation.3 | async-start | bytes 5308416 | tf_op jit(solution)/shard_map/all_to_all | solution.py:115
  66.2 59.2 %all-to-all-done.3 = bf16[320,3,8,144]{0,3,1,2:T(8,128)(2,1)} async-done(((bf16[320,3,8,144]{0,3,1,2:T(8,128)(2,1)}), bf16[320,3,8,144]{0,3,1,2:T(8,128)(2,1)}, u32[]{:S(2)}, u32[]{:S(2)}) %all-to-all-start.3) | async-done | bytes 2211872 | tf_op jit(solution)/shard_map/all_to_all | solution.py:115
  125.4 3.9 %copy.28 = bf16[8,320,3,1,144]{1,0,4,2,3:T(8,128)(2,1)} copy(bf16[8,320,3,1,144]{1,4,2,0,3:T(8,128)(2,1)} %bitcast.20) | data formatting | bytes 4423680 | tf_op jit(solution)/shard_map/all_to_all | solution.py:115
  129.4 5.2 %reshape.160 = bf16[2560,3,144]{0,2,1:T(8,128)(2,1)} reshape(bf16[8,320,3,1,144]{1,0,4,2,3:T(8,128)(2,1)} %copy.28) | data formatting | bytes 4423680 | tf_op jit(solution)/shard_map/reshape | solution.py:119
  134.6 3.0 %fusion.84 = (bf16[2560,1,144]{0,2,1:T(8,128)(2,1)}, bf16[2560,1,144]{0,2,1:T(8,128)(2,1)}, bf16[2560,1,144]{0,2,1:T(8,128)(2,1)}) fusion(bf16[2560,3,144]{0,2,1:T(8,128)(2,1)} %reshape.160), kind=kLoop, calls=%fused_computation.116 | loop fusion | bytes 4423680 | tf_op jit(solution)/shard_map/slice | solution.py:43
  137.6 68.0 %while.10 = (s32[]{:T(128)}, bf16[5,512,144]{1,2,0:T(8,128)(2,1)}, s32[5]{0:T(128)S(1)}, s32[2560]{0:T(1024)S(1)}, bf16[2560,2,72]{0,2,1:T(8,128)(2,1)}, /*index...) while((s32[]{:T(128)}, bf16[5,512,144]{1,2,0:T(8,128)(2,1)}, ...), condition=%wide.region_10.11_spmd, body=%wide.region_7.10_spmd.sunk | while | flops 785266688 | bytes 38802096 | solution.py:65
  138.9 0.8 broadcast_compare_fusion.2
  139.7 3.7 %fusion.103 = (f32[2,512]{1,0:T(2,128)S(1)}, f32[2,512,2560]{2,1,0:T(8,128)S(1)}) fusion(pred[512,2560]{1,0:T(8,128)(4,1)S(1)} %broadcast_compare_fusion.2, bf16[2560,2,72]{0,2,1:T(8,128)(2,1)} %get-tuple-element.142, bf16[2560,2,72]{0,2,1:T(8,128)(2,1)} %get-tuple-element.141, s32[]{:T(128)S(6)} %select_n.87), kind=kOutput, calls=%fused_computation.7.clone.1 | convolution fusion | flops 385350656 | bytes 12685316 | tf_op jit(solution)/shard_map/while/body/eval_jaxpr/qhd,khd->hqk/dot_general | solution.py:52
  143.4 3.0 %fusion.104 = f32[2,512]{1,0:T(2,128)S(1)} fusion(f32[2,512,2560]{2,1,0:T(8,128)S(1)} %get-tuple-element.113, f32[2,512]{1,0:T(2,128)S(1)} %get-tuple-element.114, pred[512,2560]{1,0:T(8,128)(4,1)S(1)} %broadcast_compare_fusion.2), kind=kLoop, calls=%fused_computation.8.clone.1 | loop fusion | flops 10484736 | bytes 11804672 | tf_op jit(solution)/shard_map/while/body/eval_jaxpr/reduce_sum | solution.py:59
  146.4 4.1 %fusion.105 = bf16[512,2,72]{0,2,1:T(8,128)(2,1)S(1)} fusion(bf16[2560,2,72]{0,2,1:T(8,128)(2,1)} %get-tuple-element.143, f32[2,512,2560]{2,1,0:T(8,128)S(1)} %get-tuple-element.113, f32[2,512]{1,0:T(2,128)S(1)} %get-tuple-element.114, pred[512,2560]{1,0:T(8,128)(4,1)S(1)} %broadcast_compare_fusion.2, f32[512,2]{0,1:T(2,128)S(1)} %bitcast.182), kind=kOutput, calls=%fused_computation.15.clone.1 | convolution fusion | flops 388120576 | bytes 12689408 | tf_op jit(solution)/shard_map/while/body/eval_jaxpr/hqk,khd->qhd/dot_general | solution.py:61
  150.5 0.7 constant_dynamic-update-slice_fusion.2
  152.5 0.8 broadcast_compare_fusion.2
  153.3 3.7 %fusion.103 = (f32[2,512]{1,0:T(2,128)S(1)}, f32[2,512,2560]{2,1,0:T(8,128)S(1)}) fusion(pred[512,2560]{1,0:T(8,128)(4,1)S(1)} %broadcast_compare_fusion.2, bf16[2560,2,72]{0,2,1:T(8,128)(2,1)} %get-tuple-element.142, bf16[2560,2,72]{0,2,1:T(8,128)(2,1)} %get-tuple-element.141, s32[]{:T(128)S(6)} %select_n.87), kind=kOutput, calls=%fused_computation.7.clone.1 | convolution fusion | flops 385350656 | bytes 12685316 | tf_op jit(solution)/shard_map/while/body/eval_jaxpr/qhd,khd->hqk/dot_general | solution.py:52
  157.0 3.0 %fusion.104 = f32[2,512]{1,0:T(2,128)S(1)} fusion(f32[2,512,2560]{2,1,0:T(8,128)S(1)} %get-tuple-element.113, f32[2,512]{1,0:T(2,128)S(1)} %get-tuple-element.114, pred[512,2560]{1,0:T(8,128)(4,1)S(1)} %broadcast_compare_fusion.2), kind=kLoop, calls=%fused_computation.8.clone.1 | loop fusion | flops 10484736 | bytes 11804672 | tf_op jit(solution)/shard_map/while/body/eval_jaxpr/reduce_sum | solution.py:59
  160.1 4.1 %fusion.105 = bf16[512,2,72]{0,2,1:T(8,128)(2,1)S(1)} fusion(bf16[2560,2,72]{0,2,1:T(8,128)(2,1)} %get-tuple-element.143, f32[2,512,2560]{2,1,0:T(8,128)S(1)} %get-tuple-element.113, f32[2,512]{1,0:T(2,128)S(1)} %get-tuple-element.114, pred[512,2560]{1,0:T(8,128)(4,1)S(1)} %broadcast_compare_fusion.2, f32[512,2]{0,1:T(2,128)S(1)} %bitcast.182), kind=kOutput, calls=%fused_computation.15.clone.1 | convolution fusion | flops 388120576 | bytes 12689408 | tf_op jit(solution)/shard_map/while/body/eval_jaxpr/hqk,khd->qhd/dot_general | solution.py:61
  166.1 0.8 broadcast_compare_fusion.2
  166.9 3.7 %fusion.103 = (f32[2,512]{1,0:T(2,128)S(1)}, f32[2,512,2560]{2,1,0:T(8,128)S(1)}) fusion(pred[512,2560]{1,0:T(8,128)(4,1)S(1)} %broadcast_compare_fusion.2, bf16[2560,2,72]{0,2,1:T(8,128)(2,1)} %get-tuple-element.142, bf16[2560,2,72]{0,2,1:T(8,128)(2,1)} %get-tuple-element.141, s32[]{:T(128)S(6)} %select_n.87), kind=kOutput, calls=%fused_computation.7.clone.1 | convolution fusion | flops 385350656 | bytes 12685316 | tf_op jit(solution)/shard_map/while/body/eval_jaxpr/qhd,khd->hqk/dot_general | solution.py:52
  170.6 3.0 %fusion.104 = f32[2,512]{1,0:T(2,128)S(1)} fusion(f32[2,512,2560]{2,1,0:T(8,128)S(1)} %get-tuple-element.113, f32[2,512]{1,0:T(2,128)S(1)} %get-tuple-element.114, pred[512,2560]{1,0:T(8,128)(4,1)S(1)} %broadcast_compare_fusion.2), kind=kLoop, calls=%fused_computation.8.clone.1 | loop fusion | flops 10484736 | bytes 11804672 | tf_op jit(solution)/shard_map/while/body/eval_jaxpr/reduce_sum | solution.py:59
  173.7 4.1 %fusion.105 = bf16[512,2,72]{0,2,1:T(8,128)(2,1)S(1)} fusion(bf16[2560,2,72]{0,2,1:T(8,128)(2,1)} %get-tuple-element.143, f32[2,512,2560]{2,1,0:T(8,128)S(1)} %get-tuple-element.113, f32[2,512]{1,0:T(2,128)S(1)} %get-tuple-element.114, pred[512,2560]{1,0:T(8,128)(4,1)S(1)} %broadcast_compare_fusion.2, f32[512,2]{0,1:T(2,128)S(1)} %bitcast.182), kind=kOutput, calls=%fused_computation.15.clone.1 | convolution fusion | flops 388120576 | bytes 12689408 | tf_op jit(solution)/shard_map/while/body/eval_jaxpr/hqk,khd->qhd/dot_general | solution.py:61
  179.7 0.8 broadcast_compare_fusion.2
  180.5 3.7 %fusion.103 = (f32[2,512]{1,0:T(2,128)S(1)}, f32[2,512,2560]{2,1,0:T(8,128)S(1)}) fusion(pred[512,2560]{1,0:T(8,128)(4,1)S(1)} %broadcast_compare_fusion.2, bf16[2560,2,72]{0,2,1:T(8,128)(2,1)} %get-tuple-element.142, bf16[2560,2,72]{0,2,1:T(8,128)(2,1)} %get-tuple-element.141, s32[]{:T(128)S(6)} %select_n.87), kind=kOutput, calls=%fused_computation.7.clone.1 | convolution fusion | flops 385350656 | bytes 12685316 | tf_op jit(solution)/shard_map/while/body/eval_jaxpr/qhd,khd->hqk/dot_general | solution.py:52
  184.2 3.0 %fusion.104 = f32[2,512]{1,0:T(2,128)S(1)} fusion(f32[2,512,2560]{2,1,0:T(8,128)S(1)} %get-tuple-element.113, f32[2,512]{1,0:T(2,128)S(1)} %get-tuple-element.114, pred[512,2560]{1,0:T(8,128)(4,1)S(1)} %broadcast_compare_fusion.2), kind=kLoop, calls=%fused_computation.8.clone.1 | loop fusion | flops 10484736 | bytes 11804672 | tf_op jit(solution)/shard_map/while/body/eval_jaxpr/reduce_sum | solution.py:59
  187.3 4.1 %fusion.105 = bf16[512,2,72]{0,2,1:T(8,128)(2,1)S(1)} fusion(bf16[2560,2,72]{0,2,1:T(8,128)(2,1)} %get-tuple-element.143, f32[2,512,2560]{2,1,0:T(8,128)S(1)} %get-tuple-element.113, f32[2,512]{1,0:T(2,128)S(1)} %get-tuple-element.114, pred[512,2560]{1,0:T(8,128)(4,1)S(1)} %broadcast_compare_fusion.2, f32[512,2]{0,1:T(2,128)S(1)} %bitcast.182), kind=kOutput, calls=%fused_computation.15.clone.1 | convolution fusion | flops 388120576 | bytes 12689408 | tf_op jit(solution)/shard_map/while/body/eval_jaxpr/hqk,khd->qhd/dot_general | solution.py:61
  193.3 0.8 broadcast_compare_fusion.2
  194.1 3.7 %fusion.103 = (f32[2,512]{1,0:T(2,128)S(1)}, f32[2,512,2560]{2,1,0:T(8,128)S(1)}) fusion(pred[512,2560]{1,0:T(8,128)(4,1)S(1)} %broadcast_compare_fusion.2, bf16[2560,2,72]{0,2,1:T(8,128)(2,1)} %get-tuple-element.142, bf16[2560,2,72]{0,2,1:T(8,128)(2,1)} %get-tuple-element.141, s32[]{:T(128)S(6)} %select_n.87), kind=kOutput, calls=%fused_computation.7.clone.1 | convolution fusion | flops 385350656 | bytes 12685316 | tf_op jit(solution)/shard_map/while/body/eval_jaxpr/qhd,khd->hqk/dot_general | solution.py:52
  197.8 3.0 %fusion.104 = f32[2,512]{1,0:T(2,128)S(1)} fusion(f32[2,512,2560]{2,1,0:T(8,128)S(1)} %get-tuple-element.113, f32[2,512]{1,0:T(2,128)S(1)} %get-tuple-element.114, pred[512,2560]{1,0:T(8,128)(4,1)S(1)} %broadcast_compare_fusion.2), kind=kLoop, calls=%fused_computation.8.clone.1 | loop fusion | flops 10484736 | bytes 11804672 | tf_op jit(solution)/shard_map/while/body/eval_jaxpr/reduce_sum | solution.py:59
  200.9 4.1 %fusion.105 = bf16[512,2,72]{0,2,1:T(8,128)(2,1)S(1)} fusion(bf16[2560,2,72]{0,2,1:T(8,128)(2,1)} %get-tuple-element.143, f32[2,512,2560]{2,1,0:T(8,128)S(1)} %get-tuple-element.113, f32[2,512]{1,0:T(2,128)S(1)} %get-tuple-element.114, pred[512,2560]{1,0:T(8,128)(4,1)S(1)} %broadcast_compare_fusion.2, f32[512,2]{0,1:T(2,128)S(1)} %bitcast.182), kind=kOutput, calls=%fused_computation.15.clone.1 | convolution fusion | flops 388120576 | bytes 12689408 | tf_op jit(solution)/shard_map/while/body/eval_jaxpr/hqk,khd->qhd/dot_general | solution.py:61
  205.6 2.6 copy.29
  208.3 2.8 %reshape_reshape.6 = bf16[2560,1,144]{0,2,1:T(8,128)(2,1)} reshape(bf16[5,512,144]{1,0,2:T(8,128)(2,1)} %copy.29) | data formatting | bytes 1474560 | tf_op jit(solution)/shard_map/reshape;reshape | solution.py:124
  211.1 0.9 fusion.66
  212.0 1.0 fusion.65
  213.0 0.9 fusion.64
  213.9 1.0 fusion.63
  215.0 0.9 fusion.62
  215.9 1.0 fusion.61
  216.9 0.9 fusion.60
  217.8 1.0 fusion.59
  218.8 26.3 %all_to_all.60 = bf16[8,320,1,144]{1,3,2,0:T(8,128)(2,1)S(1)} all-to-all(bf16[8,320,1,144]{1,3,2,0:T(8,128)(2,1)S(1)} %fusion.59), channel_id=1, replica_groups=mesh['bag'=4,'sp'=8] {'sp'}, dimensions={0} | all-to-all | bytes 1474560 | tf_op jit(solution)/shard_map/all_to_all | solution.py:122
  245.2 2.8 %fusion.85 = (f32[320]{0:T(512)S(1)}, f32[320,1152]{1,0:T(8,128)S(1)}) fusion(bf16[320,1152]{0,1:T(8,128)(2,1)S(1)} %bitcast.176, bf16[1152,1152]{1,0:T(8,128)(2,1)S(1)} %copy-done, f32[320,6,1152]{2,0,1:T(8,128)} %fusion.67, bf16[320,1152]{1,0:T(8,128)(2,1)S(1)} %bitcast.173), kind=kOutput, calls=%fused_computation.117 | convolution fusion | flops 851558080 | bytes 7079168 | tf_op jit(solution)/shard_map/dot_general | solution.py:70
  248.0 1.2 copy-done.4
  249.5 11.4 %fusion.30 = bf16[320,1152]{1,0:T(8,128)(2,1)} fusion(f32[320,1152]{1,0:T(8,128)} %copy-done.4, bf16[2304,1152]{1,0:T(8,128)(2,1)} %param.15, f32[320,6,1152]{2,0,1:T(8,128)} %fusion.67, bf16[1152,2304]{1,0:T(8,128)(2,1)} %param.14, f32[320]{0:T(512)S(1)} %add_rsqrt_fusion, f32[320]{0:T(512)S(1)} %broadcast_multiply_fusion), kind=kOutput, calls=%fused_computation.36 | convolution fusion | flops 3407339520 | bytes 18729472 | tf_op jit(solution)/shard_map/dot_general | solution.py:80
  260.9 3.5 %all-to-all-start.5 = ((bf16[4,80,1152]{2,1,0:T(8,128)(2,1)}), bf16[4,80,1152]{2,1,0:T(8,128)(2,1)S(1)}, u32[]{:S(2)}, u32[]{:S(2)}) async-start(bf16[4,80,1152]{2,1,0:T(8,128)(2,1)} %bitcast.181), calls=%async_computation.5 | async-start | bytes 1474560 | tf_op jit(solution)/shard_map/all_to_all | solution.py:133
  264.4 11.0 %all-to-all-done.5 = bf16[4,80,1152]{2,1,0:T(8,128)(2,1)S(1)} async-done(((bf16[4,80,1152]{2,1,0:T(8,128)(2,1)}), bf16[4,80,1152]{2,1,0:T(8,128)(2,1)S(1)}, u32[]{:S(2)}, u32[]{:S(2)}) %all-to-all-start.5) | async-done | bytes 737312 | tf_op jit(solution)/shard_map/all_to_all | solution.py:133
  275.4 2.1 gather_fusion.2
  277.5 2.0 broadcast_select_fusion
  (62 shorter events, 10.0 us)
Async XLA Ops:
  0.0 245.2 %copy-start = (bf16[1152,1152]{1,0:T(8,128)(2,1)S(1)}, bf16[1152,1152]{1,0:T(8,128)(2,1)}, u32[]{:S(2)}) copy-start(bf16[1152,1152]{1,0:T(8,128)(2,1)} %param.13) | copy-start | bytes 7962628
  0.0 15.5 %copy-start.1 = (bf16[256,1152]{1,0:T(8,128)(2,1)S(1)}, bf16[256,1152]{1,0:T(8,128)(2,1)}, u32[]{:S(2)}) copy-start(bf16[256,1152]{1,0:T(8,128)(2,1)} %param.9) | copy-start | bytes 1769476
  11.1 9.4 %all-to-all-start.1 = ((bf16[4,80,1]{1,2,0:T(2,128)(2,1)}), bf16[4,80,1]{1,2,0:T(2,128)(2,1)S(1)}, u32[]{:S(2)}, u32[]{:S(2)}) async-start(bf16[4,80,1]{1,2,0:T(2,128)(2,1)} %all_to_all.53), calls=%async_computation.1 | async-start | bytes 4096 | tf_op jit(solution)/shard_map/all_to_all | solution.py:107
  18.2 7.8 %copy-start.5 = (f32[4,6,1152]{2,0,1:T(4,128)S(1)}, f32[4,6,1152]{2,0,1:T(4,128)}, u32[]{:S(2)}) copy-start(f32[4,6,1152]{2,0,1:T(4,128)} %param.11) | copy-start | bytes 331780
  20.5 14.6 %all-to-all-start = ((bf16[4,80,1152]{2,1,0:T(8,128)(2,1)}), bf16[4,80,1152]{2,1,0:T(8,128)(2,1)S(1)}, u32[]{:S(2)}, u32[]{:S(2)}) async-start(bf16[4,80,1152]{2,1,0:T(8,128)(2,1)} %select_select_fusion), calls=%async_computation | async-start | bytes 1474560 | tf_op jit(solution)/shard_map/all_to_all | solution.py:106
  35.0 9.3 %copy-start.2 = (bf16[4,80,1152]{2,1,0:T(8,128)(2,1)}, bf16[4,80,1152]{2,1,0:T(8,128)(2,1)S(1)}, u32[]{:S(2)}) copy-start(bf16[4,80,1152]{2,1,0:T(8,128)(2,1)S(1)} %all-to-all-done) | copy-start | bytes 2211844
  35.0 25.0 %all-to-all-start.2 = ((bf16[8,2,160]{2,1,0:T(2,128)(2,1)}), bf16[8,2,160]{2,1,0:T(2,128)(2,1)S(1)}, u32[]{:S(2)}, u32[]{:S(2)}) async-start(bf16[8,2,160]{2,1,0:T(2,128)(2,1)} %reshape.216), calls=%async_computation.2 | async-start | bytes 16384 | tf_op jit(solution)/shard_map/all_to_all | solution.py:116
  60.0 65.4 %all-to-all-start.3 = ((bf16[320,3,8,144]{0,3,1,2:T(8,128)(2,1)}), bf16[320,3,8,144]{0,3,1,2:T(8,128)(2,1)}, u32[]{:S(2)}, u32[]{:S(2)}) async-start(bf16[320,3,8,144]{0,3,1,2:T(8,128)(2,1)} %copy.27), calls=%async_computation.3 | async-start | bytes 5308416 | tf_op jit(solution)/shard_map/all_to_all | solution.py:115
  208.3 36.9 %copy-start.3 = (bf16[4,80,1152]{2,1,0:T(8,128)(2,1)S(1)}, bf16[4,80,1152]{2,1,0:T(8,128)(2,1)}, u32[]{:S(2)}) copy-start(bf16[4,80,1152]{2,1,0:T(8,128)(2,1)} %copy-done.2) | copy-start | bytes 2211844
  248.0 1.2 copy-start.4
  260.9 14.6 %all-to-all-start.5 = ((bf16[4,80,1152]{2,1,0:T(8,128)(2,1)}), bf16[4,80,1152]{2,1,0:T(8,128)(2,1)S(1)}, u32[]{:S(2)}, u32[]{:S(2)}) async-start(bf16[4,80,1152]{2,1,0:T(8,128)(2,1)} %bitcast.181), calls=%async_computation.5 | async-start | bytes 1474560 | tf_op jit(solution)/shard_map/all_to_all | solution.py:133
